TPU v7x, 256 devices: a whole 4x4x8 slice. The times are simulated.
256 devices in a mesh: dp: 8 (over y, core), expert: 32 (over x, z).
Axes of the slice: x: 4, y: 4, z: 8, core: 2. Of those that a mesh axis runs over, the one named last changes fastest.
Arguments:
- tokens: bfloat16 [32768, 2048], P(('dp', 'expert')), may hold values from -6 to 6
- expert_ids: int32 [32768, 2], P(('dp', 'expert')), may hold values from 0 to 31, all different within a row; in each aligned block of 128 rows (0 to 127, 128 to 255, ...) at most 12 rows name the same one
- upstream: bfloat16 [32768, 2048], P(('dp', 'expert')), may hold values from -6 to 6
- gain: float32 [2048], replicated, may hold values from 0.5 to 1.5
- router: bfloat16 [2048, 32], replicated, may hold values from -0.125 to 0.125
- gate_weight_matrix: bfloat16 [32, 2048, 1024], P('expert', 'dp'), may hold values from -0.125 to 0.125
- up_weight: bfloat16 [32, 2048, 1024], P('expert', 'dp'), may hold values from -0.125 to 0.125
- down_weight: bfloat16 [32, 1024, 2048], P('expert', None, 'dp'), may hold values from -0.1875 to 0.1875
Outputs:
- mixed: bfloat16 [32768, 2048], P(('dp', 'expert'))
- d_tokens: bfloat16 [32768, 2048], P(('dp', 'expert'))
- gate_weight_gradient: bfloat16 [32, 2048, 1024], P('expert', 'dp')
- up_weight_gradient: bfloat16 [32, 2048, 1024], P('expert', 'dp')
- down_weight_gradient: bfloat16 [32, 1024, 2048], P('expert', None, 'dp')
- d_router: float32 [2048, 32], replicated
- d_gain: float32 [2048], replicated
Inputs may be any that keep to these rules, and one draw needn't show every extreme that they name: `expert_ids`: the two experts of a token differ. Among the tokens of one device (aligned blocks of 128 rows) no expert is named more than 12 times, and in some block one expert is named exactly 12 times.
All inputs are finite; a program needn't handle non-finite values.
Results may differ from a plain program's by a relative error of at most 0.014.
Values may be sent and summed in bfloat16 or wider, within the bound.
No kernel may reach another device: no remote copies, remote signals or barrier semaphores. Data moves between devices by JAX's collectives and lax.ppermute only.
A program may use at most 128 MiB of HBM per device.

v0:
```python
import jax
import jax.numpy as jnp
from jax import lax
from jax.sharding import PartitionSpec as P

norm_eps = 1e-06


def slot_layout(expert_ids, experts, capacity):
    flattened = expert_ids.reshape(-1)
    onehot = (flattened[:, None] == jnp.arange(experts, dtype=jnp.int32)[None, :]).astype(jnp.int32)
    ranking = jnp.sum(jnp.cumsum(onehot, axis=0) * onehot, axis=1) - 1
    slot_ids = flattened * capacity + ranking
    sources = (
        jnp.zeros((experts * capacity,), jnp.int32)
        .at[slot_ids]
        .set(jnp.arange(flattened.shape[0], dtype=jnp.int32))
    )
    counts = jnp.sum(onehot, axis=0)
    slots_occupied = (jnp.arange(capacity, dtype=jnp.int32)[None, :] < counts[:, None]).reshape(-1)
    return (slot_ids, sources, slots_occupied)


def transposed_product(left, right):
    return lax.dot_general(
        left, right, (((1,), (1,)), ((), ())), preferred_element_type=jnp.float32
    )


def inner_product(left, right):
    return lax.dot_general(
        left, right, (((0,), (0,)), ((), ())), preferred_element_type=jnp.float32
    )


def on_device(
    tokens, expert_ids, upstream, gain, router, gate_weight_matrix, up_weight, down_weight
):
    experts = lax.axis_size("expert")
    tok_rows = tokens.shape[0]
    width = tokens.shape[1]
    feed = gate_weight_matrix.shape[2]
    capacity = 3 * tok_rows // experts
    source = tokens.astype(jnp.float32)
    inverse = lax.rsqrt(jnp.mean(source * source, axis=-1, keepdims=True) + norm_eps)
    unit_rows = source * inverse
    normed = (unit_rows * gain).astype(jnp.bfloat16)
    scores = jax.nn.sigmoid(jnp.dot(normed, router, preferred_element_type=jnp.float32))
    picked = expert_ids[:, :, None] == jnp.arange(experts, dtype=jnp.int32)[None, None, :]
    chosen = jnp.sum(jnp.where(picked, scores[:, None, :], 0.0), axis=2)
    total = jnp.sum(chosen, axis=1, keepdims=True)
    gates = chosen / total
    slot_ids, sources, slots_occupied = slot_layout(expert_ids, experts, capacity)
    slot_pairs = slot_ids.reshape(tok_rows, 2)
    send_rows = jnp.where(
        slots_occupied[:, None], normed[sources // 2], jnp.zeros((), jnp.bfloat16)
    )
    arrived = lax.all_to_all(
        send_rows.reshape(experts, capacity, width),
        "expert",
        split_axis=0,
        concat_axis=0,
        tiled=True,
    )
    expert_in = arrived.reshape(experts * capacity, width)
    pieces = (
        lax.all_gather(gate_weight_matrix, "dp", axis=1, tiled=True),
        lax.all_gather(up_weight, "dp", axis=1, tiled=True),
    )
    columns = expert_in
    pre_gate = jnp.dot(columns, pieces[0][0], preferred_element_type=jnp.float32)
    pre_up = jnp.dot(columns, pieces[1][0], preferred_element_type=jnp.float32)
    sigma = jax.nn.sigmoid(pre_gate)
    active = pre_gate * sigma
    hidden = (active * pre_up).astype(jnp.bfloat16)
    expert_out = jnp.dot(
        hidden,
        lax.all_gather(down_weight, "dp", axis=2, tiled=True)[0],
        preferred_element_type=jnp.float32,
    ).astype(jnp.bfloat16)
    returned = lax.all_to_all(
        expert_out.reshape(experts, capacity, width),
        "expert",
        split_axis=0,
        concat_axis=0,
        tiled=True,
    )
    outputs = returned.reshape(experts * capacity, width)[slot_pairs].astype(jnp.float32)
    combined = gates[:, :, None] * outputs
    mixed = (source + combined[:, 0] + combined[:, 1]).astype(jnp.bfloat16)
    cotangent = upstream.astype(jnp.float32)
    d_gates = jnp.sum(cotangent[:, None, :] * outputs, axis=2)
    weight_rows = gates.reshape(-1)[sources]
    d_send = jnp.where(
        slots_occupied[:, None], weight_rows[:, None] * cotangent[sources // 2], 0.0
    ).astype(jnp.bfloat16)
    d_arrived = lax.all_to_all(
        d_send.reshape(experts, capacity, width), "expert", split_axis=0, concat_axis=0, tiled=True
    )
    d_out = d_arrived.reshape(experts * capacity, width)
    columns = d_out
    d_hidden = transposed_product(columns, lax.all_gather(down_weight, "dp", axis=2, tiled=True)[0])
    d_pre_gate = (d_hidden * pre_up * sigma * (1.0 + pre_gate * (1.0 - sigma))).astype(jnp.bfloat16)
    d_pre_up = (d_hidden * active).astype(jnp.bfloat16)
    pieces = (
        lax.all_gather(gate_weight_matrix, "dp", axis=1, tiled=True),
        lax.all_gather(up_weight, "dp", axis=1, tiled=True),
    )
    block = transposed_product(d_pre_gate, pieces[0][0]) + transposed_product(
        d_pre_up, pieces[1][0]
    )
    d_rows = block.astype(jnp.bfloat16)
    d_back = lax.all_to_all(
        d_rows.reshape(experts, capacity, width), "expert", split_axis=0, concat_axis=0, tiled=True
    )
    d_parts = d_back.reshape(experts * capacity, width)[slot_pairs].astype(jnp.float32)
    grad_rows = lax.psum_scatter(
        jnp.concatenate(
            [
                inner_product(expert_in, d_pre_gate),
                inner_product(expert_in, d_pre_up),
                inner_product(d_out, hidden),
            ],
            axis=1,
        ).astype(jnp.bfloat16),
        "dp",
        scatter_dimension=0,
        tiled=True,
    ).astype(jnp.float32)
    gate_weight_gradient = grad_rows[:, :feed].astype(jnp.bfloat16)[None]
    up_weight_gradient = grad_rows[:, feed : 2 * feed].astype(jnp.bfloat16)[None]
    down_weight_gradient = grad_rows[:, 2 * feed :].T.astype(jnp.bfloat16)[None]
    blended = jnp.sum(gates * d_gates, axis=1, keepdims=True)
    d_chosen = (d_gates - blended) / total
    d_logit = d_chosen * chosen * (1.0 - chosen)
    d_logits = jnp.sum(jnp.where(picked, d_logit[:, :, None], 0.0), axis=1)
    router_float = router.astype(jnp.float32)
    d_normed = (
        d_parts[:, 0]
        + d_parts[:, 1]
        + jnp.dot(d_logits, router_float.T, precision=lax.Precision.HIGHEST)
    )
    d_unit = d_normed * gain
    inner = jnp.mean(d_unit * unit_rows, axis=-1, keepdims=True)
    d_tokens = (cotangent + inverse * (d_unit - unit_rows * inner)).astype(jnp.bfloat16)
    part_router = jnp.dot(normed.astype(jnp.float32).T, d_logits, precision=lax.Precision.HIGHEST)
    part_gain = jnp.sum(d_normed * unit_rows, axis=0)
    d_router, d_gain = lax.psum((part_router, part_gain), ("dp", "expert"))
    return (
        mixed,
        d_tokens,
        gate_weight_gradient,
        up_weight_gradient,
        down_weight_gradient,
        d_router,
        d_gain,
    )


def solution(mesh):
    return jax.shard_map(
        on_device,
        mesh=mesh,
        in_specs=(
            P(("dp", "expert"), None),
            P(("dp", "expert"), None),
            P(("dp", "expert"), None),
            P(),
            P(),
            P("expert", "dp", None),
            P("expert", "dp", None),
            P("expert", None, "dp"),
        ),
        out_specs=(
            P(("dp", "expert"), None),
            P(("dp", "expert"), None),
            P("expert", "dp", None),
            P("expert", "dp", None),
            P("expert", None, "dp"),
            P(),
            P(),
        ),
        check_vma=False,
    )
```

profile of v0, /device:TPU:2, one launch (start us, length us, event | category | flops | bytes accessed | tf_op | source)
XLA Modules:
  0.0 638.8 jit_solution(4836383149556349928)
XLA Ops:
  13.7 3.1 gather_fusion
  19.5 60.0 %all_to_all.20 = bf16[32,12,2048]{2,1,0:T(8,128)(2,1)S(1)} all-to-all(bf16[32,12,2048]{2,1,0:T(8,128)(2,1)S(1)} %broadcast_select_fusion), channel_id=1, replica_groups=mesh['dp'=8,'expert'=32] {'expert'}, dimensions={0} | all-to-all | bytes 3145728 | tf_op jit(solution)/shard_map/all_to_all | solution.py:58
  80.9 5.8 fusion.10
  86.6 5.9 multiply_convert_fusion.2
  92.6 31.3 %all-gather.8.cloned.1.call-done = bf16[1,1024,2048]{2,1,0:T(8,128)(2,1)} async-done(((bf16[1,1024,256]{2,1,0:T(8,128)(2,1)}), bf16[1,1024,2048]{2,1,0:T(8,128)(2,1)}) %all-gather.8.cloned.1.call-update) | async-done | bytes 4194320 | tf_op jit(solution)/shard_map/all_gather | solution.py:78
  123.9 4.2 fusion.14
  129.7 10.3 %all-to-all-start.1 = ((bf16[32,12,2048]{2,1,0:T(8,128)(2,1)}), bf16[32,12,2048]{2,1,0:T(8,128)(2,1)}, u32[]{:S(2)}, u32[]{:S(2)}) async-start(bf16[32,12,2048]{2,1,0:T(8,128)(2,1)} %reshape.197), calls=%async_computation.1 | async-start | bytes 4194304 | tf_op jit(solution)/shard_map/all_to_all | solution.py:81
  140.6 3.3 gather_fusion.3
  143.9 4.6 gather.24
  148.9 39.2 %all-to-all-done.1 = bf16[32,12,2048]{2,1,0:T(8,128)(2,1)} async-done(((bf16[32,12,2048]{2,1,0:T(8,128)(2,1)}), bf16[32,12,2048]{2,1,0:T(8,128)(2,1)}, u32[]{:S(2)}, u32[]{:S(2)}) %all-to-all-start.1) | async-done | bytes 1572896 | tf_op jit(solution)/shard_map/all_to_all | solution.py:81
  193.0 3.4 reshape.257
  196.3 2.6 multiply_reduce_fusion
  199.3 2.8 gather_fusion.2
  202.2 2.6 select_convert_fusion
  204.9 57.8 %all_to_all.21 = bf16[32,12,2048]{2,1,0:T(8,128)(2,1)S(1)} all-to-all(bf16[32,12,2048]{2,1,0:T(8,128)(2,1)S(1)} %select_convert_fusion), channel_id=1, replica_groups=mesh['dp'=8,'expert'=32] {'expert'}, dimensions={0} | all-to-all | bytes 3145728 | tf_op jit(solution)/shard_map/all_to_all | solution.py:97
  264.0 4.1 convolution_convert_fusion
  275.4 21.4 %pad_maximum_fusion = bf16[2048,3072]{0,1:T(8,128)(2,1)} fusion(bf16[2048,1024]{0,1:T(8,128)(2,1)S(1)} %convolution_convert_fusion, bf16[2048,1024]{0,1:T(8,128)(2,1)S(1)} %convolution_convert_fusion.1, bf16[2048,1024]{0,1:T(8,128)(2,1)S(1)} %convolution_convert_fusion.2), kind=kLoop, calls=%fused_computation.6 | loop fusion | flops 37748736 | bytes 25165824 | tf_op jit(solution)/shard_map/concatenate | solution.py:118
  297.9 4.2 fusion.4
  305.5 7.8 %all-to-all-start.3 = ((bf16[32,12,2048]{2,1,0:T(8,128)(2,1)}), bf16[32,12,2048]{2,1,0:T(8,128)(2,1)}, u32[]{:S(2)}, u32[]{:S(2)}) async-start(bf16[32,12,2048]{2,1,0:T(8,128)(2,1)} %reshape.200), calls=%async_computation.3 | async-start | bytes 4194304 | tf_op jit(solution)/shard_map/all_to_all | solution.py:113
  317.0 43.3 %all-to-all-done.3 = bf16[32,12,2048]{2,1,0:T(8,128)(2,1)} async-done(((bf16[32,12,2048]{2,1,0:T(8,128)(2,1)}), bf16[32,12,2048]{2,1,0:T(8,128)(2,1)}, u32[]{:S(2)}, u32[]{:S(2)}) %all-to-all-start.3) | async-done | bytes 1572896 | tf_op jit(solution)/shard_map/all_to_all | solution.py:113
  360.3 2.7 reshape.201
  369.7 74.9 %psum.15 = f32[2048]{0:T(1024)} all-reduce(f32[2048]{0:T(1024)S(1)} %get-tuple-element.35), channel_id=1, replica_groups=mesh['dp'=8,'expert'=32] {'dp','expert'}, use_global_device_ids=true, to_apply=%region_15.16 | all-reduce | flops 2048 | bytes 16384 | tf_op jit(solution)/shard_map/psum | solution.py:148
  444.7 2.7 fusion.30
  451.7 178.7 %all-reduce.2.cloned.1.call-done = f32[2048,32]{0,1:T(8,128)} async-done(((f32[2048,32]{0,1:T(8,128)}), f32[2048,32]{0,1:T(8,128)}) %all-reduce.2.cloned.1.call-update) | async-done | bytes 262160 | tf_op jit(solution)/shard_map/psum | solution.py:148
  (110 shorter events, 47.5 us)
Async XLA Ops:
  7.2 141.4 %copy-start = (bf16[2048,32]{0,1:T(8,128)(2,1)S(1)}, bf16[2048,32]{0,1:T(8,128)(2,1)}, u32[]{:S(2)}) copy-start(bf16[2048,32]{0,1:T(8,128)(2,1)} %param.12) | copy-start | bytes 393220
  7.2 6.1 copy-start.3
  7.2 6.3 copy-start.10
  7.2 73.7 %all-gather.4.cloned.1.call-start = ((), (), s32[]{:S(2)}) async-start(), calls=%async_computation.5 | async-start | bytes 4718592 | tf_op jit(solution)/shard_map/all_gather | solution.py:67
  7.9 78.7 %all-gather.6.cloned.1.call-start = ((), (), s32[]{:S(2)}) async-start(), calls=%async_computation.6 | async-start | bytes 4718592 | tf_op jit(solution)/shard_map/all_gather | solution.py:68
  8.7 115.2 %all-gather.8.cloned.1.call-start = ((), (), s32[]{:S(2)}) async-start(), calls=%async_computation.7 | async-start | bytes 4718592 | tf_op jit(solution)/shard_map/all_gather | solution.py:78
  80.9 5.8 copy-start.7
  129.7 10.8 %copy-start.5 = (bf16[128,2048]{1,0:T(8,128)(2,1)S(1)}, bf16[128,2048]{1,0:T(8,128)(2,1)}, u32[]{:S(2)}) copy-start(bf16[128,2048]{1,0:T(8,128)(2,1)} %param.10) | copy-start | bytes 1572868
  129.7 58.4 %all-to-all-start.1 = ((bf16[32,12,2048]{2,1,0:T(8,128)(2,1)}), bf16[32,12,2048]{2,1,0:T(8,128)(2,1)}, u32[]{:S(2)}, u32[]{:S(2)}) async-start(bf16[32,12,2048]{2,1,0:T(8,128)(2,1)} %reshape.197), calls=%async_computation.1 | async-start | bytes 4194304 | tf_op jit(solution)/shard_map/all_to_all | solution.py:81
  140.0 307.4 %reduce-scatter.2.cloned.1.call-start = ((), (), s32[]{:S(2)}) async-start(), calls=%async_computation.8 | async-start | bytes 14155776 | tf_op jit(solution)/shard_map/reduce_scatter | solution.py:117
  143.9 4.9 copy-start.11
  264.0 4.2 copy-start.9
  264.0 4.2 copy-start.13
  264.0 4.2 copy-start.18
  264.0 4.3 copy-start.19
  270.5 2.4 copy-start.14
  270.6 2.4 copy-start.16
  297.9 4.2 copy-start.12
  297.9 4.2 copy-start.15
  305.5 8.9 %copy-start.1 = (f32[128,2,2048]{2,1,0:T(2,128)S(1)}, f32[128,2,2048]{2,1,0:T(2,128)}, u32[]{:S(2)}) copy-start(f32[128,2,2048]{2,1,0:T(2,128)} %reshape.257) | copy-start | bytes 6291460
  305.5 54.9 %all-to-all-start.3 = ((bf16[32,12,2048]{2,1,0:T(8,128)(2,1)}), bf16[32,12,2048]{2,1,0:T(8,128)(2,1)}, u32[]{:S(2)}, u32[]{:S(2)}) async-start(bf16[32,12,2048]{2,1,0:T(8,128)(2,1)} %reshape.200), calls=%async_computation.3 | async-start | bytes 4194304 | tf_op jit(solution)/shard_map/all_to_all | solution.py:113
  313.3 317.1 %all-reduce.2.cloned.1.call-start = ((), (), s32[]{:S(2)}) async-start(), calls=%async_computation.9 | async-start | bytes 524288 | tf_op jit(solution)/shard_map/psum | solution.py:148
  367.4 77.3 %copy-start.2 = (f32[128,2,2048]{2,0,1:T(8,128)S(1)}, f32[128,2,2048]{2,0,1:T(8,128)}, u32[]{:S(2)}) copy-start(f32[128,2,2048]{2,0,1:T(8,128)} %copy_multiply_fusion) | copy-start | bytes 6291460
  367.4 77.3 %copy-start.6 = (bf16[128,2048]{1,0:T(8,128)(2,1)S(1)}, bf16[128,2048]{1,0:T(8,128)(2,1)}, u32[]{:S(2)}) copy-start(bf16[128,2048]{1,0:T(8,128)(2,1)} %param.10) | copy-start | bytes 1572868
  (3 other events, 5.1 us)
Sparse Core Ops, SparseCore 0:
  9.9 37.5 all-gather.3
  49.3 34.5 all-gather.5
  85.8 38.0 all-gather.7
  296.9 73.3 reduce-scatter.1
  376.2 254.0 all-reduce.1
where the time goes:
time: 646 us; the launch traced here: 639 us
  waiting for transfers between devices  295 us (46%)
  blocking collectives  193 us (30%)
  local copies, waits for them, and re-layouts  48 us (7%)
  matrix products  36.7 us (6%)
  other arithmetic  33.7 us (5%)
  starting transfers between devices  18.6 us (3%)
  between operations  14.5 us (2%)
    psum x1, waiting for transfers between devices, on_device(): d_router, d_gain = lax.psum((part_router, part_gain), ('dp', 'expert'))  179 us
    psum x1, blocking collectives, on_device(): d_router, d_gain = lax.psum((part_router, part_gain), ('dp', 'expert'))  74.9 us
    all_to_all x1, blocking collectives, on_device(): lax.all_to_all(send_rows.reshape(experts, capacity, width), 'expert', spl...  60 us
    all_to_all x1, blocking collectives, on_device(): lax.all_to_all(d_send.reshape(experts, capacity, width), 'expert', split_...  57.8 us
    all_to_all x1, waiting for transfers between devices, on_device(): lax.all_to_all(d_rows.reshape(experts, capacity, width), 'expert', split_...  43.3 us
    all_to_all x1, waiting for transfers between devices, on_device(): lax.all_to_all(expert_out.reshape(experts, capacity, width), 'expert', sp...  39.2 us
    all_gather x1, waiting for transfers between devices, on_device(): lax.all_gather(down_weight, 'dp', axis=2, tiled=True)[0]  31.3 us
    concatenate x1, other arithmetic, on_device(): jnp.concatenate([inner_product(expert_in, d_pre_gate), inner_product(expe...  21.4 us
  transfers between devices with their start and end apart: 7, of which 4 were waited for; matrix products, arithmetic and copies ran while one was open for 9% of the time, Pallas kernels for 0%

commit v1 on v0

--- a/solution.py
+++ b/solution.py
@@ -145,7 +145,8 @@
     d_tokens = (cotangent + inverse * (d_unit - unit_rows * inner)).astype(jnp.bfloat16)
     part_router = jnp.dot(normed.astype(jnp.float32).T, d_logits, precision=lax.Precision.HIGHEST)
     part_gain = jnp.sum(d_normed * unit_rows, axis=0)
-    d_router, d_gain = lax.psum((part_router, part_gain), ("dp", "expert"))
+    match_view = lambda payload: lax.psum(lax.psum(payload, axis_name="expert"), axis_name="dp")
+    d_router, d_gain = match_view((part_router, part_gain))
     return (
         mixed,
         d_tokens,

time: 646 us -> 534 us (0.83)
  waiting for transfers between devices: 295 us -> 228 us
  blocking collectives: 193 us -> 136 us
  starting transfers between devices: 18.6 us -> 29.3 us
    psum x1 -> x2, waiting for transfers between devices: 179 us -> 108 us  [the longest x1 56.7 us: on_device(): lax.psum(payload, axis_name='expert')]
    all_to_all x1 -> x0, blocking collectives: 57.8 us -> none  [on_device(): lax.all_to_all(d_send.reshape(experts, capacity, width), 'expert', split_...]
    all_to_all x0 -> x1, waiting for transfers between devices: none -> 47.6 us  [on_device(): lax.all_to_all(d_send.reshape(experts, capacity, width), 'expert', split_...]
    all_to_all x1, waiting for transfers between devices: 43.3 us -> 0.01 us  [on_device(): lax.all_to_all(d_rows.reshape(experts, capacity, width), 'expert', split_...]
    all_to_all x0 -> x1, starting transfers between devices: none -> 8.84 us  [on_device(): lax.all_to_all(d_send.reshape(experts, capacity, width), 'expert', split_...]
    psum x1 -> x2, blocking collectives: 74.9 us -> 76.2 us  [the longest x1 63 us: on_device(): lax.psum(payload, axis_name='expert')]
  transfers between devices with their start and end apart: 7 -> 9, of which waited for: 4 -> 5; matrix products, arithmetic and copies ran while one was open for 9% -> 18% of each run, Pallas kernels for 0% -> 0%
where the time goes in v1:
time: 534 us; the launch traced here: 527 us
  waiting for transfers between devices  228 us (43%)
  blocking collectives  136 us (25%)
  local copies, waits for them, and re-layouts  46.8 us (9%)
  matrix products  37 us (7%)
  other arithmetic  35 us (7%)
  starting transfers between devices  29.3 us (5%)
  between operations  14.8 us (3%)
    psum x1, blocking collectives, on_device(): lax.psum(payload, axis_name='expert')  63 us
    all_to_all x1, blocking collectives, on_device(): lax.all_to_all(send_rows.reshape(experts, capacity, width), 'expert', spl...  60 us
    psum x1, waiting for transfers between devices, on_device(): lax.psum(payload, axis_name='expert')  56.7 us
    psum x1, waiting for transfers between devices, on_device(): lax.psum(lax.psum(payload, axis_name='expert'), axis_name='dp')  50.8 us
    all_to_all x1, waiting for transfers between devices, on_device(): lax.all_to_all(d_send.reshape(experts, capacity, width), 'expert', split_...  47.6 us
    all_to_all x1, waiting for transfers between devices, on_device(): lax.all_to_all(expert_out.reshape(experts, capacity, width), 'expert', sp...  39.4 us
    all_gather x1, waiting for transfers between devices, on_device(): lax.all_gather(down_weight, 'dp', axis=2, tiled=True)[0]  31.2 us
    concatenate x1, other arithmetic, on_device(): jnp.concatenate([inner_product(expert_in, d_pre_gate), inner_product(expe...  21.4 us
  transfers between devices with their start and end apart: 9, of which 5 were waited for; matrix products, arithmetic and copies ran while one was open for 18% of the time, Pallas kernels for 0%

profile of v1, /device:TPU:2, one launch (start us, length us, event | category | flops | bytes accessed | tf_op | source)
XLA Modules:
  0.0 527.0 jit_solution(8401883406964677082)
XLA Ops:
  13.7 3.1 gather_fusion
  19.5 60.0 %all_to_all.20 = bf16[32,12,2048]{2,1,0:T(8,128)(2,1)S(1)} all-to-all(bf16[32,12,2048]{2,1,0:T(8,128)(2,1)S(1)} %broadcast_select_fusion), channel_id=1, replica_groups=mesh['dp'=8,'expert'=32] {'expert'}, dimensions={0} | all-to-all | bytes 3145728 | tf_op jit(solution)/shard_map/all_to_all | solution.py:58
  80.9 5.8 %fusion.10 = f32[384,1024]{1,0:T(8,128)} fusion(bf16[384,2048]{1,0:T(8,128)(2,1)} %reshape.196, bf16[1,2048,1024]{2,1,0:T(8,128)(2,1)} %all-gather.4.cloned.1.call-done), kind=kOutput, calls=%fused_computation.17 | convolution fusion | flops 1610612736 | bytes 7340032 | tf_op jit(solution)/shard_map/dot_general | solution.py:71
  86.6 6.0 %multiply_convert_fusion.2 = (bf16[384,1024]{1,0:T(8,128)(2,1)}, f32[384,1024]{1,0:T(8,128)}) fusion(f32[384,1024]{1,0:T(8,128)} %fusion.10, bf16[384,2048]{1,0:T(8,128)(2,1)S(1)} %copy-done.7, bf16[1,2048,1024]{2,1,0:T(8,128)(2,1)} %all-gather.6.cloned.1.call-done), kind=kOutput, calls=%fused_computation.31 | convolution fusion | flops 1612972032 | bytes 9699328 | tf_op jit(solution)/shard_map/dot_general | solution.py:72
  92.6 31.2 %all-gather.8.cloned.1.call-done = bf16[1,1024,2048]{2,1,0:T(8,128)(2,1)} async-done(((bf16[1,1024,256]{2,1,0:T(8,128)(2,1)}), bf16[1,1024,2048]{2,1,0:T(8,128)(2,1)}) %all-gather.8.cloned.1.call-update) | async-done | bytes 4194320 | tf_op jit(solution)/shard_map/all_gather | solution.py:78
  123.9 4.2 fusion.14
  129.7 10.8 %all-to-all-start.1 = ((bf16[32,12,2048]{2,1,0:T(8,128)(2,1)}), bf16[32,12,2048]{2,1,0:T(8,128)(2,1)}, u32[]{:S(2)}, u32[]{:S(2)}) async-start(bf16[32,12,2048]{2,1,0:T(8,128)(2,1)} %reshape.197), calls=%async_computation.1 | async-start | bytes 4194304 | tf_op jit(solution)/shard_map/all_to_all | solution.py:81
  140.7 3.3 gather_fusion.3
  144.0 4.6 gather.24
  148.9 39.4 %all-to-all-done.1 = bf16[32,12,2048]{2,1,0:T(8,128)(2,1)} async-done(((bf16[32,12,2048]{2,1,0:T(8,128)(2,1)}), bf16[32,12,2048]{2,1,0:T(8,128)(2,1)}, u32[]{:S(2)}, u32[]{:S(2)}) %all-to-all-start.1) | async-done | bytes 1572896 | tf_op jit(solution)/shard_map/all_to_all | solution.py:81
  193.2 3.4 reshape.257
  199.5 2.8 gather_fusion.2
  202.5 4.0 select_convert_fusion
  206.5 8.8 %all-to-all-start.2 = ((bf16[32,12,2048]{2,1,0:T(8,128)(2,1)}), bf16[32,12,2048]{2,1,0:T(8,128)(2,1)S(1)}, u32[]{:S(2)}, u32[]{:S(2)}) async-start(bf16[32,12,2048]{2,1,0:T(8,128)(2,1)} %select_convert_fusion), calls=%async_computation.2 | async-start | bytes 4194304 | tf_op jit(solution)/shard_map/all_to_all | solution.py:97
  217.0 47.6 %all-to-all-done.2 = bf16[32,12,2048]{2,1,0:T(8,128)(2,1)S(1)} async-done(((bf16[32,12,2048]{2,1,0:T(8,128)(2,1)}), bf16[32,12,2048]{2,1,0:T(8,128)(2,1)S(1)}, u32[]{:S(2)}, u32[]{:S(2)}) %all-to-all-start.2) | async-done | bytes 1572896 | tf_op jit(solution)/shard_map/all_to_all | solution.py:97
  266.0 4.1 convolution_convert_fusion
  277.4 21.4 %pad_maximum_fusion = bf16[2048,3072]{0,1:T(8,128)(2,1)} fusion(bf16[2048,1024]{0,1:T(8,128)(2,1)S(1)} %convolution_convert_fusion, bf16[2048,1024]{0,1:T(8,128)(2,1)S(1)} %convolution_convert_fusion.1, bf16[2048,1024]{0,1:T(8,128)(2,1)S(1)} %convolution_convert_fusion.2), kind=kLoop, calls=%fused_computation.6 | loop fusion | flops 37748736 | bytes 25165824 | tf_op jit(solution)/shard_map/concatenate | solution.py:118
  298.8 4.2 fusion.4
  306.4 8.9 %all-to-all-start.3 = ((bf16[32,12,2048]{2,1,0:T(8,128)(2,1)}), bf16[32,12,2048]{2,1,0:T(8,128)(2,1)}, u32[]{:S(2)}, u32[]{:S(2)}) async-start(bf16[32,12,2048]{2,1,0:T(8,128)(2,1)} %reshape.200), calls=%async_computation.3 | async-start | bytes 4194304 | tf_op jit(solution)/shard_map/all_to_all | solution.py:113
  318.0 56.7 %all-reduce.3.cloned.1.call-done = f32[2048,32]{0,1:T(8,128)} async-done(((f32[2048,32]{0,1:T(8,128)}), f32[2048,32]{0,1:T(8,128)}) %all-reduce.3.cloned.1.call-update) | async-done | bytes 262160 | tf_op jit(solution)/shard_map/psum | solution.py:148
  374.7 2.7 reshape.201
  384.2 63.0 %psum.30 = f32[2048]{0:T(1024)S(1)} all-reduce(f32[2048]{0:T(1024)S(1)} %get-tuple-element.35), channel_id=1, replica_groups=mesh['dp'=8,'expert'=32] {'expert'}, use_global_device_ids=true, to_apply=%region_16.17 | all-reduce | flops 2048 | bytes 16384 | tf_op jit(solution)/shard_map/psum | solution.py:148
  447.2 13.2 %psum.31 = f32[2048]{0:T(1024)} all-reduce(f32[2048]{0:T(1024)S(1)} %psum.30), channel_id=1, replica_groups=mesh['dp'=8,'expert'=32] {'dp'}, use_global_device_ids=true, to_apply=%region_17.18 | all-reduce | flops 2048 | bytes 16384 | tf_op jit(solution)/shard_map/psum | solution.py:148
  467.4 50.8 %all-reduce.5.cloned.1.call-done = f32[2048,32]{0,1:T(8,128)} async-done(((f32[2048,32]{0,1:T(8,128)}), f32[2048,32]{0,1:T(8,128)}) %all-reduce.5.cloned.1.call-update) | async-done | bytes 262160 | tf_op jit(solution)/shard_map/psum | solution.py:148
  (107 shorter events, 52.1 us)
Async XLA Ops:
  7.2 141.4 %copy-start = (bf16[2048,32]{0,1:T(8,128)(2,1)S(1)}, bf16[2048,32]{0,1:T(8,128)(2,1)}, u32[]{:S(2)}) copy-start(bf16[2048,32]{0,1:T(8,128)(2,1)} %param.12) | copy-start | bytes 393220
  7.2 6.1 %copy-start.3 = (bf16[128,2048]{1,0:T(8,128)(2,1)S(1)}, bf16[128,2048]{1,0:T(8,128)(2,1)}, u32[]{:S(2)}) copy-start(bf16[128,2048]{1,0:T(8,128)(2,1)} %param.8) | copy-start | bytes 1572868
  7.2 6.3 %copy-start.10 = (f32[2048]{0:T(1024)S(1)}, f32[2048]{0:T(1024)}, u32[]{:S(2)}) copy-start(f32[2048]{0:T(1024)} %param.11) | copy-start | bytes 24580
  7.2 73.7 %all-gather.4.cloned.1.call-start = ((), (), s32[]{:S(2)}) async-start(), calls=%async_computation.5 | async-start | bytes 4718592 | tf_op jit(solution)/shard_map/all_gather | solution.py:67
  7.9 78.7 %all-gather.6.cloned.1.call-start = ((), (), s32[]{:S(2)}) async-start(), calls=%async_computation.6 | async-start | bytes 4718592 | tf_op jit(solution)/shard_map/all_gather | solution.py:68
  8.7 115.2 %all-gather.8.cloned.1.call-start = ((), (), s32[]{:S(2)}) async-start(), calls=%async_computation.7 | async-start | bytes 4718592 | tf_op jit(solution)/shard_map/all_gather | solution.py:78
  80.9 5.8 %copy-start.7 = (bf16[384,2048]{1,0:T(8,128)(2,1)S(1)}, bf16[384,2048]{1,0:T(8,128)(2,1)}, u32[]{:S(2)}) copy-start(bf16[384,2048]{1,0:T(8,128)(2,1)} %reshape.196) | copy-start | bytes 4718596
  129.7 11.0 %copy-start.5 = (bf16[128,2048]{1,0:T(8,128)(2,1)S(1)}, bf16[128,2048]{1,0:T(8,128)(2,1)}, u32[]{:S(2)}) copy-start(bf16[128,2048]{1,0:T(8,128)(2,1)} %param.10) | copy-start | bytes 1572868
  129.7 58.7 %all-to-all-start.1 = ((bf16[32,12,2048]{2,1,0:T(8,128)(2,1)}), bf16[32,12,2048]{2,1,0:T(8,128)(2,1)}, u32[]{:S(2)}, u32[]{:S(2)}) async-start(bf16[32,12,2048]{2,1,0:T(8,128)(2,1)} %reshape.197), calls=%async_computation.1 | async-start | bytes 4194304 | tf_op jit(solution)/shard_map/all_to_all | solution.py:81
  144.0 4.9 copy-start.11
  206.5 58.2 %all-to-all-start.2 = ((bf16[32,12,2048]{2,1,0:T(8,128)(2,1)}), bf16[32,12,2048]{2,1,0:T(8,128)(2,1)S(1)}, u32[]{:S(2)}, u32[]{:S(2)}) async-start(bf16[32,12,2048]{2,1,0:T(8,128)(2,1)} %select_convert_fusion), calls=%async_computation.2 | async-start | bytes 4194304 | tf_op jit(solution)/shard_map/all_to_all | solution.py:97
  215.3 159.4 %all-reduce.3.cloned.1.call-start = ((), (), s32[]{:S(2)}) async-start(), calls=%async_computation.9 | async-start | bytes 524288 | tf_op jit(solution)/shard_map/psum | solution.py:148
  216.5 246.7 %reduce-scatter.2.cloned.1.call-start = ((), (), s32[]{:S(2)}) async-start(), calls=%async_computation.8 | async-start | bytes 14155776 | tf_op jit(solution)/shard_map/reduce_scatter | solution.py:117
  266.0 4.2 copy-start.9
  266.0 4.2 copy-start.13
  266.0 4.2 copy-start.14
  266.0 4.3 copy-start.15
  270.3 2.3 copy-start.8
  298.8 4.2 copy-start.12
  306.4 9.0 %copy-start.1 = (f32[128,2,2048]{2,1,0:T(2,128)S(1)}, f32[128,2,2048]{2,1,0:T(2,128)}, u32[]{:S(2)}) copy-start(f32[128,2,2048]{2,1,0:T(2,128)} %reshape.257) | copy-start | bytes 6291460
  306.4 68.3 %all-to-all-start.3 = ((bf16[32,12,2048]{2,1,0:T(8,128)(2,1)}), bf16[32,12,2048]{2,1,0:T(8,128)(2,1)}, u32[]{:S(2)}, u32[]{:S(2)}) async-start(bf16[32,12,2048]{2,1,0:T(8,128)(2,1)} %reshape.200), calls=%async_computation.3 | async-start | bytes 4194304 | tf_op jit(solution)/shard_map/all_to_all | solution.py:113
  315.3 202.9 %all-reduce.5.cloned.1.call-start = ((), (), s32[]{:S(2)}) async-start(), calls=%async_computation.10 | async-start | bytes 524288 | tf_op jit(solution)/shard_map/psum | solution.py:148
  381.8 78.7 %copy-start.2 = (f32[128,2,2048]{2,0,1:T(8,128)S(1)}, f32[128,2,2048]{2,0,1:T(8,128)}, u32[]{:S(2)}) copy-start(f32[128,2,2048]{2,0,1:T(8,128)} %copy_multiply_fusion) | copy-start | bytes 6291460
  381.8 78.6 %copy-start.6 = (bf16[128,2048]{1,0:T(8,128)(2,1)S(1)}, bf16[128,2048]{1,0:T(8,128)(2,1)}, u32[]{:S(2)}) copy-start(bf16[128,2048]{1,0:T(8,128)(2,1)} %param.10) | copy-start | bytes 1572868
  (1 other events, 1.7 us)
Sparse Core Ops, SparseCore 0:
  9.9 37.5 all-gather.3
  49.3 34.5 all-gather.5
  85.8 38.0 all-gather.7
  219.8 154.7 all-reduce.2
  377.1 73.7 reduce-scatter.1
  453.0 65.1 all-reduce.4
